TPU v7x, 32 devices: a whole 2x2x4 slice. The times are simulated.
32 devices in a mesh: group: 2 (over y), tile: 4 (over z), col: 2 (over x), layer: 2 (over core).
Axes of the slice: x: 2, y: 2, z: 4, core: 2. Of those that a mesh axis runs over, the one named last changes fastest.
Arguments:
- source: float32 [4, 40, 96, 512], P('group', 'layer', 'tile', 'col'), parts along dimension 0, may hold values from -12 to 12
- profile: float32 [40], P('layer'), may hold values from 0.5 to 1
- column: float32 [192, 512], P(('group', 'tile'), 'col'), parts along dimension 0, may hold values from 0.6 to 1.2
- terrain_height_error: int32 [4, 96, 512], P('group', 'tile', 'col'), parts along dimension 0, may hold values from -150 to 149
Outputs:
- solution: float32 [4, 40, 96, 512], P('group', 'layer', 'tile', 'col'), parts along dimension 0
There are 2 independent parts, one for each index of `group`. A program takes and returns all parts, laid end to end along the dimension named above; an argument that names none is the same for every part. Nothing has to cross between parts.
All inputs are finite; a program needn't handle non-finite values.
Results may differ from a plain program's by a relative error of at most 0.0001.
Values sent between devices are 32-bit elements; how exact they have to be, the bound alone decides.
No kernel may reach another device: no remote copies, remote signals or barrier semaphores. Data moves between devices by JAX's collectives and lax.ppermute only.
A program may use at most 64 MiB of HBM per device.

v0:
```python
import jax
import jax.numpy as jnp
from jax import lax
from jax.sharding import PartitionSpec as P

ITERS = 2
weight_horiz = 1.0
weight_vert = 2.0
weight_cross = 0.3
gain_bound = 1.6
total_weight = 10.4
diag_shift = 0.5
source_scale = 8.0


def padded_2(shard, sides, width):
    for axis, dim in sides:
        count, length = (lax.axis_size(axis), shard.shape[dim])
        up = [(i, (i + 1) % count) for i in range(count - 1)]
        down = [(j, i) for i, j in up]
        last = lax.slice_in_dim(shard, length - width, length, axis=dim)
        initial = lax.slice_in_dim(shard, 0, width, axis=dim)
        before = lax.ppermute(last, axis, up)
        after = lax.ppermute(initial, axis, down)
        shard = jnp.concatenate([before, shard, after], axis=dim)
    return shard


def stencil_sum(padded):
    horiz = (
        padded[:, 1:-1, 2:, 1:-1]
        + padded[:, 1:-1, :-2, 1:-1]
        + padded[:, 1:-1, 1:-1, 2:]
        + padded[:, 1:-1, 1:-1, :-2]
    )
    vert = padded[:, 2:, 1:-1, 1:-1] + padded[:, :-2, 1:-1, 1:-1]
    cross = (
        padded[:, 2:, 2:, 1:-1]
        + padded[:, 2:, :-2, 1:-1]
        + padded[:, :-2, 2:, 1:-1]
        + padded[:, :-2, :-2, 1:-1]
    )
    cross = (
        cross
        + padded[:, 2:, 1:-1, 2:]
        + padded[:, 2:, 1:-1, :-2]
        + padded[:, :-2, 1:-1, 2:]
        + padded[:, :-2, 1:-1, :-2]
    )
    return weight_horiz * horiz + weight_vert * vert + weight_cross * cross


def apply_operator(field, metric, diag_full):
    weighted = metric * field
    vertical = padded_2(weighted, (("layer", 1),), 1)
    padded = padded_2(vertical, (("tile", 2), ("col", 3)), 1)
    return diag_full * field - metric * stencil_sum(padded)


def error_spread(values):
    return values[:, None, None, None]


def local(source, profile, column, terrain_height_error):
    multiplier_factor = 1.0 + 0.002 * terrain_height_error.astype(jnp.float32)
    metric = (
        profile[None, :, None, None] * column[None, None, :, :] * multiplier_factor[:, None, :, :]
    )
    diag_full = gain_bound * total_weight * metric + diag_shift
    forcing_term = source_scale * metric * source
    residual = forcing_term
    scaled = forcing_term / diag_full
    applied = apply_operator(scaled, metric, diag_full)
    solution = jnp.zeros_like(forcing_term)
    direction = jnp.zeros_like(forcing_term)
    search_img = jnp.zeros_like(forcing_term)
    preconditioned_direction = jnp.zeros_like(forcing_term)
    img_dir = jnp.zeros_like(forcing_term)
    gamma_old = None
    alpha_old = None
    for step in range(ITERS):
        gamma_now, delta_now = lax.psum(
            (jnp.sum(residual * scaled, axis=(1, 2, 3)), jnp.sum(applied * scaled, axis=(1, 2, 3))),
            ("tile", "col", "layer"),
        )
        if step == 0:
            beta_now = jnp.zeros_like(gamma_now)
            alpha_now = gamma_now / delta_now
        else:
            beta_now = gamma_now / gamma_old
            alpha_now = gamma_now / (delta_now - beta_now * gamma_now / alpha_old)
        direction = scaled + error_spread(beta_now) * direction
        solution = solution + error_spread(alpha_now) * direction
        if step + 1 < ITERS:
            pre_app = applied / diag_full
            preconditioned_image = apply_operator(pre_app, metric, diag_full)
            img_dir = preconditioned_image + error_spread(beta_now) * img_dir
            preconditioned_direction = pre_app + error_spread(beta_now) * preconditioned_direction
            search_img = applied + error_spread(beta_now) * search_img
            residual = residual - error_spread(alpha_now) * search_img
            scaled = scaled - error_spread(alpha_now) * preconditioned_direction
            applied = applied - error_spread(alpha_now) * img_dir
        gamma_old = gamma_now
        alpha_old = alpha_now
    return solution


def solution(mesh):
    placed = (
        P("group", "layer", "tile", "col"),
        P("layer"),
        P(("group", "tile"), "col"),
        P("group", "tile", "col"),
    )
    return jax.shard_map(
        local,
        mesh=mesh,
        in_specs=placed,
        out_specs=P("group", "layer", "tile", "col"),
        check_vma=False,
    )
```

profile of v0, /device:TPU:0, one launch (start us, length us, event | category | flops | bytes accessed | tf_op | source)
XLA Modules:
  0.0 139.2 jit_solution(2850471159662051467)
XLA Ops:
  1.6 1.5 %multiply_multiply_fusion.3 = f32[2,20,24,256]{3,2,1,0:T(8,128)S(1)} fusion(f32[2,24,256]{2,1,0:T(8,128)S(1)} %multiply_add_fusion.1, f32[20,24,256]{2,1,0:T(8,128)S(1)} %broadcast_multiply_fusion, f32[2,20,24,256]{3,2,1,0:T(8,128)} %param.4), kind=kLoop, calls=%fused_computation.3 | loop fusion | flops 1720320 | bytes 2506752 | tf_op jit(solution)/shard_map/mul | solution.py:54
  3.1 2.4 %collective-permute-start = (f32[2,1,24,256]{3,2,1,0:T(8,128)S(1)}, f32[2,1,24,256]{3,2,1,0:T(8,128)S(1)}, u32[]{:S(2)}, u32[]{:S(2)}) collective-permute-start(f32[2,1,24,256]{3,2,1,0:T(8,128)S(1)} %get-tuple-element.33), channel_id=1, source_target_pairs={{0,1},{2,3},{4,5},{6,7},{8,9},{10,11},{12,13},{14,15},{16,17},{18,... | collective-permute-start | bytes 147464 | tf_op jit(solution)/shard_map/ppermute | solution.py:23
  5.5 1.3 collective-permute-start.1
  6.9 1.8 %collective-permute-done.1 = f32[2,1,24,256]{3,2,1,0:T(8,128)S(1)} collective-permute-done((f32[2,1,24,256]{3,2,1,0:T(8,128)S(1)}, f32[2,1,24,256]{3,2,1,0:T(8,128)S(1)}, u32[]{:S(2)}, u32[]{:S(2)}) %collective-permute-start.1) | collective-permute-done | bytes 49184 | tf_op jit(solution)/shard_map/ppermute | solution.py:24
  8.8 1.3 collective-permute-start.2
  10.1 4.9 %collective-permute-start.3 = (f32[2,22,1,256]{3,1,2,0:T(8,128)S(1)}, f32[2,22,1,256]{3,1,2,0:T(8,128)S(1)}, u32[]{:S(2)}, u32[]{:S(2)}) collective-permute-start(f32[2,22,1,256]{3,1,2,0:T(8,128)S(1)} %copy.72), channel_id=1, source_target_pairs={{0,4},{4,8},{8,12},{1,5},{5,9},{9,13},{2,6},{6,10},{10,14},{3,7},{... | collective-permute-start | bytes 135176 | tf_op jit(solution)/shard_map/ppermute | solution.py:23
  15.2 1.6 %collective-permute-done.3 = f32[2,22,1,256]{3,1,2,0:T(8,128)S(1)} collective-permute-done((f32[2,22,1,256]{3,1,2,0:T(8,128)S(1)}, f32[2,22,1,256]{3,1,2,0:T(8,128)S(1)}, u32[]{:S(2)}, u32[]{:S(2)}) %collective-permute-start.3) | collective-permute-done | bytes 45088 | tf_op jit(solution)/shard_map/ppermute | solution.py:23
  18.1 3.8 %collective-permute-start.5 = (f32[2,22,26,1]{2,1,3,0:T(8,128)S(1)}, f32[2,22,26,1]{2,1,3,0:T(8,128)S(1)}, u32[]{:S(2)}, u32[]{:S(2)}) collective-permute-start(f32[2,22,26,1]{2,1,3,0:T(8,128)S(1)} %copy.59), channel_id=1, source_target_pairs={{0,2},{1,3},{4,6},{5,7},{8,10},{9,11},{12,14},{13,15},{16,18},{17,... | collective-permute-start | bytes 13736 | tf_op jit(solution)/shard_map/ppermute | solution.py:23
  21.9 1.3 collective-permute-start.4
  23.2 1.9 %pad_maximum_fusion.2 = (f32[2,22,25,256]{3,2,1,0:T(8,128)}, f32[2,22,25,256]{3,2,1,0:T(8,128)}) fusion(f32[2,22,1,256]{3,2,1,0:T(1,128)S(1)} %copy.52, f32[2,1,24,256]{3,2,1,0:T(8,128)S(1)} %collective-permute-done.1, f32[2,20,24,256]{3,2,1,0:T(8,128)S(1)} %multiply_multiply_fusion.3, f32[2,1,24,256]{3,2,1,0:T(8,128)S(1)} %collective-permute-done, ...), kind=kLoop, calls=%fused_computation.10 | loop fusion | flops 1689600 | bytes 3424256 | tf_op jit(solution)/shard_map/concatenate | solution.py:25
  25.1 2.5 %collective-permute-done.4 = f32[2,22,26,1]{2,1,3,0:T(8,128)S(1)} collective-permute-done((f32[2,22,26,1]{2,1,3,0:T(8,128)S(1)}, f32[2,22,26,1]{2,1,3,0:T(8,128)S(1)}, u32[]{:S(2)}, u32[]{:S(2)}) %collective-permute-start.4) | collective-permute-done | bytes 4608 | tf_op jit(solution)/shard_map/ppermute | solution.py:24
  28.0 1.3 copy.60
  29.3 2.8 %pad_maximum_fusion = (f32[2,22,26,257]{3,2,1,0:T(8,128)S(1)}, f32[2,22,26,257]{3,2,1,0:T(8,128)S(1)}) fusion(f32[2,22,26,1]{3,2,1,0:T(8,128)S(1)} %copy.58, f32[2,22,1,256]{3,2,1,0:T(1,128)S(1)} %copy.52, f32[2,1,24,256]{3,2,1,0:T(8,128)S(1)} %collective-permute-done.1, f32[2,20,24,256]{3,2,1,0:T(8,128)S(1)} %multiply_multiply_fusion.3, ...), kind=kLoop, calls=%fused_computation.6 | loop fusion | flops 2940080 | bytes 3532672 | tf_op jit(solution)/shard_map/concatenate | solution.py:25
  32.2 3.1 %multiply_multiply_fusion.1 = (f32[2,20,24,256]{3,2,1,0:T(8,128)S(1)}, f32[2,20,24,256]{3,2,1,0:T(8,128)S(1)}) fusion(f32[2,24,256]{2,1,0:T(8,128)S(1)} %multiply_add_fusion.1, f32[20,24,256]{2,1,0:T(8,128)S(1)} %broadcast_multiply_fusion, f32[2,22,26,257]{3,2,1,0:T(8,128)S(1)} %get-tuple-element.22, f32[2,22,26,257]{3,2,1,0:T(8,128)S(1)} %get-tuple-element.21, ...), kind=kLoop, calls=%fused_computation.1 | loop fusion | flops 6881280 | bytes 16367616 | tf_op jit(solution)/shard_map/mul | solution.py:54
  36.0 1.3 collective-permute-start.6
  37.3 1.3 collective-permute-start.7
  39.2 34.9 %all-reduce.1 = (f32[2]{0:T(128)S(1)}, f32[2]{0:T(128)S(1)}) all-reduce(f32[2]{0:T(128)S(1)} %get-tuple-element.6, f32[2]{0:T(128)S(1)} %get-tuple-element.5), channel_id=1, replica_groups=mesh['group'=2,'tile'=4,'col'=2,'layer'=2] {'tile','col','layer'}, use_global_device_ids=true, to_apply=%region_1.0 | all-reduce | flops 4 | bytes 32 | tf_op jit(solution)/shard_map/psum | solution.py:82
  75.0 1.3 collective-permute-start.8
  76.3 4.5 %collective-permute-start.9 = (f32[2,22,1,256]{3,1,2,0:T(8,128)S(1)}, f32[2,22,1,256]{3,1,2,0:T(8,128)S(1)}, u32[]{:S(2)}, u32[]{:S(2)}) collective-permute-start(f32[2,22,1,256]{3,1,2,0:T(8,128)S(1)} %copy.74), channel_id=1, source_target_pairs={{0,4},{4,8},{8,12},{1,5},{5,9},{9,13},{2,6},{6,10},{10,14},{3,7},{... | collective-permute-start | bytes 135176 | tf_op jit(solution)/shard_map/ppermute | solution.py:23
  83.7 1.4 fusion.23
  85.0 2.1 %copy.67 = f32[2,22,26,1]{2,1,3,0:T(8,128)} copy(f32[2,22,26,1]{3,2,1,0:T(8,128)} %get-tuple-element.15) | data formatting | bytes 9152 | tf_op jit(solution)/shard_map/slice | solution.py:22
  87.1 2.1 %copy.69 = f32[2,22,26,1]{2,1,3,0:T(8,128)} copy(f32[2,22,26,1]{3,2,1,0:T(8,128)} %get-tuple-element.16) | data formatting | bytes 9152 | tf_op jit(solution)/shard_map/slice | solution.py:21
  89.2 1.9 %collective-permute-start.11 = (f32[2,22,26,1]{2,1,3,0:T(8,128)}, f32[2,22,26,1]{2,1,3,0:T(8,128)}, u32[]{:S(2)}, u32[]{:S(2)}) collective-permute-start(f32[2,22,26,1]{2,1,3,0:T(8,128)} %copy.69), channel_id=1, source_target_pairs={{0,2},{1,3},{4,6},{5,7},{8,10},{9,11},{12,14},{13,15},{16,18},{17,... | collective-permute-start | bytes 13736 | tf_op jit(solution)/shard_map/ppermute | solution.py:23
  91.1 1.3 collective-permute-start.10
  92.4 2.8 %pad_maximum_fusion.4 = (f32[2,22,25,256]{3,2,1,0:T(8,128)}, f32[2,22,25,256]{3,2,1,0:T(8,128)}) fusion(f32[2,22,1,256]{3,2,1,0:T(1,128)} %copy-done.8, f32[2,1,24,256]{3,2,1,0:T(8,128)} %collective-permute-done.7, f32[2,20,24,256]{3,2,1,0:T(8,128)S(1)} %get-tuple-element.13, f32[2,1,24,256]{3,2,1,0:T(8,128)S(1)} %collective-permute-done.6, ...), kind=kLoop, calls=%fused_computation.13 | loop fusion | flops 1689600 | bytes 3424256 | tf_op jit(solution)/shard_map/concatenate | solution.py:25
  95.2 1.9 %collective-permute-done.10 = f32[2,22,26,1]{2,1,3,0:T(8,128)} collective-permute-done((f32[2,22,26,1]{2,1,3,0:T(8,128)}, f32[2,22,26,1]{2,1,3,0:T(8,128)}, u32[]{:S(2)}, u32[]{:S(2)}) %collective-permute-start.10) | collective-permute-done | bytes 4608 | tf_op jit(solution)/shard_map/ppermute | solution.py:24
  97.1 2.0 %copy.68 = f32[2,22,26,1]{3,2,1,0:T(8,128)} copy(f32[2,22,26,1]{2,1,3,0:T(8,128)} %collective-permute-done.10) | data formatting | bytes 9152 | tf_op jit(solution)/shard_map/ppermute | solution.py:24
  99.1 2.0 %copy.70 = f32[2,22,26,1]{3,2,1,0:T(8,128)} copy(f32[2,22,26,1]{2,1,3,0:T(8,128)} %collective-permute-done.11) | data formatting | bytes 9152 | tf_op jit(solution)/shard_map/ppermute | solution.py:23
  101.1 3.1 %pad_maximum_fusion.1 = (f32[2,22,26,257]{3,2,1,0:T(8,128)S(1)}, f32[2,22,26,257]{3,2,1,0:T(8,128)S(1)}) fusion(f32[2,22,26,1]{3,2,1,0:T(8,128)} %copy.68, f32[2,22,1,256]{3,2,1,0:T(1,128)} %copy-done.8, f32[2,1,24,256]{3,2,1,0:T(8,128)} %collective-permute-done.7, f32[2,20,24,256]{3,2,1,0:T(8,128)S(1)} %get-tuple-element.13, ...), kind=kLoop, calls=%fused_computation.8 | loop fusion | flops 2940080 | bytes 3532672 | tf_op jit(solution)/shard_map/concatenate | solution.py:25
  104.2 3.5 %fusion.11 = f32[2]{0:T(128)S(1)} fusion(f32[2,20,24,256]{3,2,1,0:T(8,128)S(1)} %copy-done.2, f32[2,22,26,257]{3,2,1,0:T(8,128)S(1)} %get-tuple-element.20, f32[2,22,26,257]{3,2,1,0:T(8,128)S(1)} %get-tuple-element.19, f32[2,22,25,256]{3,2,1,0:T(8,128)S(1)} %copy-done.6, f32[2,22,25,256]{3,2,1,0:T(8,128)S(1)} %copy-done.5, ...), kind=kLoop, calls=%fused_computation.27 | loop fusion | flops 8110078 | bytes 15384592 | tf_op jit(solution)/shard_map/reduce_sum | solution.py:83
  107.7 29.5 %all-reduce = (f32[2]{0:T(128)S(1)}, f32[2]{0:T(128)S(1)}) all-reduce(f32[2]{0:T(128)S(1)} %multiply_reduce_fusion, f32[2]{0:T(128)S(1)} %fusion.11), channel_id=1, replica_groups=mesh['group'=2,'tile'=4,'col'=2,'layer'=2] {'tile','col','layer'}, use_global_device_ids=true, to_apply=%region_5.0 | all-reduce | flops 4 | bytes 32 | tf_op jit(solution)/shard_map/psum | solution.py:82
  137.8 1.4 %multiply_add_fusion = f32[2,20,24,256]{3,2,1,0:T(8,128)} fusion(f32[2]{0:T(128)S(1)} %get-tuple-element.12, f32[2]{0:T(128)S(1)} %get-tuple-element.11, f32[2]{0:T(128)S(1)} %div.19, f32[2,20,24,256]{3,2,1,0:T(8,128)S(1)} %copy-done.2, f32[2,24,256]{2,1,0:T(8,128)S(1)} %multiply_add_fusion.1, f32[20,24,256]{2,1,0:T(8,128)S(1)} %broadcast_multiply_fusion, ...), kind=kLoop, calls=%fused_computation.62 | loop fusion | flops 3440640 | bytes 3489816 | tf_op jit(solution)/shard_map/add | solution.py:93
  (54 shorter events, 9.3 us)
Async XLA Ops:
  3.1 3.7 %collective-permute-start = (f32[2,1,24,256]{3,2,1,0:T(8,128)S(1)}, f32[2,1,24,256]{3,2,1,0:T(8,128)S(1)}, u32[]{:S(2)}, u32[]{:S(2)}) collective-permute-start(f32[2,1,24,256]{3,2,1,0:T(8,128)S(1)} %get-tuple-element.33), channel_id=1, source_target_pairs={{0,1},{2,3},{4,5},{6,7},{8,9},{10,11},{12,13},{14,15},{16,17},{18,... | collective-permute-start | bytes 147464 | tf_op jit(solution)/shard_map/ppermute | solution.py:23
  5.5 3.1 %collective-permute-start.1 = (f32[2,1,24,256]{3,2,1,0:T(8,128)S(1)}, f32[2,1,24,256]{3,2,1,0:T(8,128)S(1)}, u32[]{:S(2)}, u32[]{:S(2)}) collective-permute-start(f32[2,1,24,256]{3,2,1,0:T(8,128)S(1)} %get-tuple-element.34), channel_id=1, source_target_pairs={{1,0},{3,2},{5,4},{7,6},{9,8},{11,10},{13,12},{15,14},{17,16},{19,... | collective-permute-start | bytes 147464 | tf_op jit(solution)/shard_map/ppermute | solution.py:24
  8.7 20.6 %copy-start.7 = (f32[2,1,24,256]{3,2,1,0:T(8,128)}, f32[2,1,24,256]{3,2,1,0:T(8,128)S(1)}, u32[]{:S(2)}) copy-start(f32[2,1,24,256]{3,2,1,0:T(8,128)S(1)} %collective-permute-done.1) | copy-start | bytes 147460
  8.8 6.4 %collective-permute-start.2 = (f32[2,22,1,256]{3,1,2,0:T(8,128)S(1)}, f32[2,22,1,256]{3,1,2,0:T(8,128)S(1)}, u32[]{:S(2)}, u32[]{:S(2)}) collective-permute-start(f32[2,22,1,256]{3,1,2,0:T(8,128)S(1)} %copy.71), channel_id=1, source_target_pairs={{4,0},{8,4},{12,8},{5,1},{9,5},{13,9},{6,2},{10,6},{14,10},{7,3},{... | collective-permute-start | bytes 135176 | tf_op jit(solution)/shard_map/ppermute | solution.py:24
  10.1 6.7 %collective-permute-start.3 = (f32[2,22,1,256]{3,1,2,0:T(8,128)S(1)}, f32[2,22,1,256]{3,1,2,0:T(8,128)S(1)}, u32[]{:S(2)}, u32[]{:S(2)}) collective-permute-start(f32[2,22,1,256]{3,1,2,0:T(8,128)S(1)} %copy.72), channel_id=1, source_target_pairs={{0,4},{4,8},{8,12},{1,5},{5,9},{9,13},{2,6},{6,10},{10,14},{3,7},{... | collective-permute-start | bytes 135176 | tf_op jit(solution)/shard_map/ppermute | solution.py:23
  18.1 10.0 %collective-permute-start.5 = (f32[2,22,26,1]{2,1,3,0:T(8,128)S(1)}, f32[2,22,26,1]{2,1,3,0:T(8,128)S(1)}, u32[]{:S(2)}, u32[]{:S(2)}) collective-permute-start(f32[2,22,26,1]{2,1,3,0:T(8,128)S(1)} %copy.59), channel_id=1, source_target_pairs={{0,2},{1,3},{4,6},{5,7},{8,10},{9,11},{12,14},{13,15},{16,18},{17,... | collective-permute-start | bytes 13736 | tf_op jit(solution)/shard_map/ppermute | solution.py:23
  21.9 5.7 %collective-permute-start.4 = (f32[2,22,26,1]{2,1,3,0:T(8,128)S(1)}, f32[2,22,26,1]{2,1,3,0:T(8,128)S(1)}, u32[]{:S(2)}, u32[]{:S(2)}) collective-permute-start(f32[2,22,26,1]{2,1,3,0:T(8,128)S(1)} %copy.57), channel_id=1, source_target_pairs={{2,0},{3,1},{6,4},{7,5},{10,8},{11,9},{14,12},{15,13},{18,16},{19,... | collective-permute-start | bytes 13736 | tf_op jit(solution)/shard_map/ppermute | solution.py:24
  29.3 2.8 %copy-start = (f32[2,20,24,256]{3,2,1,0:T(8,128)S(1)}, f32[2,20,24,256]{3,2,1,0:T(8,128)}, u32[]{:S(2)}) copy-start(f32[2,20,24,256]{3,2,1,0:T(8,128)} %param.4) | copy-start | bytes 2949124
  29.3 2.9 %copy-start.3 = (f32[2,22,25,256]{3,2,1,0:T(8,128)S(1)}, f32[2,22,25,256]{3,2,1,0:T(8,128)}, u32[]{:S(2)}) copy-start(f32[2,22,25,256]{3,2,1,0:T(8,128)} %get-tuple-element.27) | copy-start | bytes 3379204
  29.3 2.9 %copy-start.4 = (f32[2,22,25,256]{3,2,1,0:T(8,128)S(1)}, f32[2,22,25,256]{3,2,1,0:T(8,128)}, u32[]{:S(2)}) copy-start(f32[2,22,25,256]{3,2,1,0:T(8,128)} %get-tuple-element.28) | copy-start | bytes 3379204
  35.3 3.3 %copy-start.1 = (f32[2,20,24,256]{3,2,1,0:T(8,128)}, f32[2,20,24,256]{3,2,1,0:T(8,128)S(1)}, u32[]{:S(2)}) copy-start(f32[2,20,24,256]{3,2,1,0:T(8,128)S(1)} %get-tuple-element.14) | copy-start | bytes 2949124
  36.0 38.1 %collective-permute-start.6 = (f32[2,1,24,256]{3,2,1,0:T(8,128)}, f32[2,1,24,256]{3,2,1,0:T(8,128)S(1)}, u32[]{:S(2)}, u32[]{:S(2)}) collective-permute-start(f32[2,1,24,256]{3,2,1,0:T(8,128)} %get-tuple-element.31), channel_id=1, source_target_pairs={{0,1},{2,3},{4,5},{6,7},{8,9},{10,11},{12,13},{14,15},{16,17},{18,... | collective-permute-start | bytes 147464 | tf_op jit(solution)/shard_map/ppermute | solution.py:23
  37.3 36.8 %collective-permute-start.7 = (f32[2,1,24,256]{3,2,1,0:T(8,128)}, f32[2,1,24,256]{3,2,1,0:T(8,128)}, u32[]{:S(2)}, u32[]{:S(2)}) collective-permute-start(f32[2,1,24,256]{3,2,1,0:T(8,128)} %get-tuple-element.32), channel_id=1, source_target_pairs={{1,0},{3,2},{5,4},{7,6},{9,8},{11,10},{13,12},{15,14},{17,16},{19,... | collective-permute-start | bytes 147464 | tf_op jit(solution)/shard_map/ppermute | solution.py:24
  39.2 41.6 %copy-start.2 = (f32[2,20,24,256]{3,2,1,0:T(8,128)S(1)}, f32[2,20,24,256]{3,2,1,0:T(8,128)}, u32[]{:S(2)}) copy-start(f32[2,20,24,256]{3,2,1,0:T(8,128)} %copy-done.1) | copy-start | bytes 2949124
  74.1 2.2 %copy-start.10 = (f32[2]{0:T(128)}, f32[2]{0:T(128)S(1)}, u32[]{:S(2)}) copy-start(f32[2]{0:T(128)S(1)} %get-tuple-element.10) | copy-start | bytes 28
  75.0 6.4 %collective-permute-start.8 = (f32[2,22,1,256]{3,1,2,0:T(8,128)S(1)}, f32[2,22,1,256]{3,1,2,0:T(8,128)S(1)}, u32[]{:S(2)}, u32[]{:S(2)}) collective-permute-start(f32[2,22,1,256]{3,1,2,0:T(8,128)S(1)} %copy.73), channel_id=1, source_target_pairs={{4,0},{8,4},{12,8},{5,1},{9,5},{13,9},{6,2},{10,6},{14,10},{7,3},{... | collective-permute-start | bytes 135176 | tf_op jit(solution)/shard_map/ppermute | solution.py:24
  76.3 6.3 %collective-permute-start.9 = (f32[2,22,1,256]{3,1,2,0:T(8,128)S(1)}, f32[2,22,1,256]{3,1,2,0:T(8,128)S(1)}, u32[]{:S(2)}, u32[]{:S(2)}) collective-permute-start(f32[2,22,1,256]{3,1,2,0:T(8,128)S(1)} %copy.74), channel_id=1, source_target_pairs={{0,4},{4,8},{8,12},{1,5},{5,9},{9,13},{2,6},{6,10},{10,14},{3,7},{... | collective-permute-start | bytes 135176 | tf_op jit(solution)/shard_map/ppermute | solution.py:23
  81.4 3.6 %copy-start.8 = (f32[2,22,1,256]{3,2,1,0:T(1,128)}, f32[2,22,1,256]{3,2,1,0:T(1,128)S(1)}, u32[]{:S(2)}) copy-start(f32[2,22,1,256]{3,2,1,0:T(1,128)S(1)} %copy.62) | copy-start | bytes 135172
  82.6 2.4 %copy-start.9 = (f32[2,22,1,256]{3,2,1,0:T(1,128)}, f32[2,22,1,256]{3,2,1,0:T(1,128)S(1)}, u32[]{:S(2)}) copy-start(f32[2,22,1,256]{3,2,1,0:T(1,128)S(1)} %copy.64) | copy-start | bytes 135172
  89.2 9.9 %collective-permute-start.11 = (f32[2,22,26,1]{2,1,3,0:T(8,128)}, f32[2,22,26,1]{2,1,3,0:T(8,128)}, u32[]{:S(2)}, u32[]{:S(2)}) collective-permute-start(f32[2,22,26,1]{2,1,3,0:T(8,128)} %copy.69), channel_id=1, source_target_pairs={{0,2},{1,3},{4,6},{5,7},{8,10},{9,11},{12,14},{13,15},{16,18},{17,... | collective-permute-start | bytes 13736 | tf_op jit(solution)/shard_map/ppermute | solution.py:23
  91.1 6.0 %collective-permute-start.10 = (f32[2,22,26,1]{2,1,3,0:T(8,128)}, f32[2,22,26,1]{2,1,3,0:T(8,128)}, u32[]{:S(2)}, u32[]{:S(2)}) collective-permute-start(f32[2,22,26,1]{2,1,3,0:T(8,128)} %copy.67), channel_id=1, source_target_pairs={{2,0},{3,1},{6,4},{7,5},{10,8},{11,9},{14,12},{15,13},{18,16},{19,... | collective-permute-start | bytes 13736 | tf_op jit(solution)/shard_map/ppermute | solution.py:24
  101.1 3.1 %copy-start.5 = (f32[2,22,25,256]{3,2,1,0:T(8,128)S(1)}, f32[2,22,25,256]{3,2,1,0:T(8,128)}, u32[]{:S(2)}) copy-start(f32[2,22,25,256]{3,2,1,0:T(8,128)} %get-tuple-element.23) | copy-start | bytes 3379204
  101.1 3.1 %copy-start.6 = (f32[2,22,25,256]{3,2,1,0:T(8,128)S(1)}, f32[2,22,25,256]{3,2,1,0:T(8,128)}, u32[]{:S(2)}) copy-start(f32[2,22,25,256]{3,2,1,0:T(8,128)} %get-tuple-element.24) | copy-start | bytes 3379204
where the time goes:
time: 140 us; the launch traced here: 139 us
  blocking collectives  64.3 us (46%)
  starting transfers between devices  26.6 us (19%)
  other arithmetic  25.8 us (18%)
  local copies, waits for them, and re-layouts  13.2 us (9%)
  waiting for transfers between devices  9.04 us (6%)
    psum x2, blocking collectives, local(): lax.psum((jnp.sum(residual * scaled, axis=(1, 2, 3)), jnp.sum(applied * s...  64.3 us
    ppermute x6, starting transfers between devices, padded_2(): before = lax.ppermute(last, axis, up)  18.9 us
    concatenate x8, other arithmetic, padded_2(): shard = jnp.concatenate([before, shard, after], axis=dim)  12.8 us
    ppermute x6, starting transfers between devices, padded_2(): after = lax.ppermute(initial, axis, down)  7.74 us
    ppermute x6, waiting for transfers between devices, padded_2(): after = lax.ppermute(initial, axis, down)  6.36 us
    mul x2, other arithmetic, apply_operator(): weighted = metric * field  4.6 us
    reduce_sum x2, other arithmetic, local(): jnp.sum(applied * scaled, axis=(1, 2, 3))  4.11 us
    slice x4, local copies, waits for them, and re-layouts, padded_2(): initial = lax.slice_in_dim(shard, 0, width, axis=dim)  4.09 us
  transfers between devices with their start and end apart: 12, of which 6 were waited for; matrix products, arithmetic and copies ran while one was open for 6% of the time, Pallas kernels for 0%

commit v1 on v0

--- a/solution.py
+++ b/solution.py
@@ -80,8 +80,14 @@
     alpha_old = None
     for step in range(ITERS):
         gamma_now, delta_now = lax.psum(
-            (jnp.sum(residual * scaled, axis=(1, 2, 3)), jnp.sum(applied * scaled, axis=(1, 2, 3))),
-            ("tile", "col", "layer"),
+            lax.psum(
+                (
+                    jnp.sum(residual * scaled, axis=(1, 2, 3)),
+                    jnp.sum(applied * scaled, axis=(1, 2, 3)),
+                ),
+                "tile",
+            ),
+            ("col", "layer"),
         )
         if step == 0:
             beta_now = jnp.zeros_like(gamma_now)

time: 140 us -> 113 us (0.81)
  blocking collectives: 64.3 us -> 35.5 us
  starting transfers between devices: 26.6 us -> 28.4 us
    psum x2, blocking collectives: 64.3 us -> 24 us  [local(): lax.psum((jnp.sum(residual * scaled, axis=(1, 2, 3)), jnp.sum(applied * s...]
    psum x0 -> x2, blocking collectives: none -> 11.5 us  [local(): lax.psum(lax.psum((jnp.sum(residual * scaled, axis=(1, 2, 3)), jnp.sum(ap...]
    ppermute x6, starting transfers between devices: 18.9 us -> 20.7 us  [padded_2(): before = lax.ppermute(last, axis, up)]
  transfers between devices with their start and end apart: 12 -> 12, of which waited for: 6 -> 6; matrix products, arithmetic and copies ran while one was open for 6% -> 8% of each run, Pallas kernels for 0% -> 0%
where the time goes in v1:
time: 113 us; the launch traced here: 112 us
  blocking collectives  35.5 us (31%)
  starting transfers between devices  28.4 us (25%)
  other arithmetic  25.8 us (23%)
  local copies, waits for them, and re-layouts  13.2 us (12%)
  waiting for transfers between devices  9 us (8%)
    psum x2, blocking collectives, local(): lax.psum((jnp.sum(residual * scaled, axis=(1, 2, 3)), jnp.sum(applied * s...  24 us
    ppermute x6, starting transfers between devices, padded_2(): before = lax.ppermute(last, axis, up)  20.7 us
    concatenate x8, other arithmetic, padded_2(): shard = jnp.concatenate([before, shard, after], axis=dim)  12.8 us
    psum x2, blocking collectives, local(): lax.psum(lax.psum((jnp.sum(residual * scaled, axis=(1, 2, 3)), jnp.sum(ap...  11.5 us
    ppermute x6, starting transfers between devices, padded_2(): after = lax.ppermute(initial, axis, down)  7.74 us
    ppermute x6, waiting for transfers between devices, padded_2(): after = lax.ppermute(initial, axis, down)  6.32 us
    mul x2, other arithmetic, apply_operator(): weighted = metric * field  4.6 us
    reduce_sum x2, other arithmetic, local(): jnp.sum(applied * scaled, axis=(1, 2, 3))  4.11 us
  transfers between devices with their start and end apart: 12, of which 6 were waited for; matrix products, arithmetic and copies ran while one was open for 8% of the time, Pallas kernels for 0%

profile of v1, /device:TPU:0, one launch (start us, length us, event | category | flops | bytes accessed | tf_op | source)
XLA Modules:
  0.0 112.3 jit_solution(6086660064796771227)
XLA Ops:
  1.6 1.5 %multiply_multiply_fusion.3 = f32[2,20,24,256]{3,2,1,0:T(8,128)S(1)} fusion(f32[2,24,256]{2,1,0:T(8,128)S(1)} %multiply_add_fusion.1, f32[20,24,256]{2,1,0:T(8,128)S(1)} %broadcast_multiply_fusion, f32[2,20,24,256]{3,2,1,0:T(8,128)} %param.4), kind=kLoop, calls=%fused_computation.3 | loop fusion | flops 1720320 | bytes 2506752 | tf_op jit(solution)/shard_map/mul | solution.py:54
  3.1 2.4 %collective-permute-start = (f32[2,1,24,256]{3,2,1,0:T(8,128)S(1)}, f32[2,1,24,256]{3,2,1,0:T(8,128)S(1)}, u32[]{:S(2)}, u32[]{:S(2)}) collective-permute-start(f32[2,1,24,256]{3,2,1,0:T(8,128)S(1)} %get-tuple-element.37), channel_id=1, source_target_pairs={{0,1},{2,3},{4,5},{6,7},{8,9},{10,11},{12,13},{14,15},{16,17},{18,... | collective-permute-start | bytes 147464 | tf_op jit(solution)/shard_map/ppermute | solution.py:23
  5.5 1.3 %collective-permute-start.1 = (f32[2,1,24,256]{3,2,1,0:T(8,128)S(1)}, f32[2,1,24,256]{3,2,1,0:T(8,128)S(1)}, u32[]{:S(2)}, u32[]{:S(2)}) collective-permute-start(f32[2,1,24,256]{3,2,1,0:T(8,128)S(1)} %get-tuple-element.38), channel_id=1, source_target_pairs={{1,0},{3,2},{5,4},{7,6},{9,8},{11,10},{13,12},{15,14},{17,16},{19,... | collective-permute-start | bytes 147464 | tf_op jit(solution)/shard_map/ppermute | solution.py:24
  6.9 1.8 %collective-permute-done.1 = f32[2,1,24,256]{3,2,1,0:T(8,128)S(1)} collective-permute-done((f32[2,1,24,256]{3,2,1,0:T(8,128)S(1)}, f32[2,1,24,256]{3,2,1,0:T(8,128)S(1)}, u32[]{:S(2)}, u32[]{:S(2)}) %collective-permute-start.1) | collective-permute-done | bytes 49184 | tf_op jit(solution)/shard_map/ppermute | solution.py:24
  8.8 1.3 %collective-permute-start.2 = (f32[2,22,1,256]{3,1,2,0:T(8,128)S(1)}, f32[2,22,1,256]{3,1,2,0:T(8,128)S(1)}, u32[]{:S(2)}, u32[]{:S(2)}) collective-permute-start(f32[2,22,1,256]{3,1,2,0:T(8,128)S(1)} %copy.71), channel_id=1, source_target_pairs={{4,0},{8,4},{12,8},{5,1},{9,5},{13,9},{6,2},{10,6},{14,10},{7,3},{... | collective-permute-start | bytes 135176 | tf_op jit(solution)/shard_map/ppermute | solution.py:24
  10.1 4.9 %collective-permute-start.3 = (f32[2,22,1,256]{3,1,2,0:T(8,128)S(1)}, f32[2,22,1,256]{3,1,2,0:T(8,128)S(1)}, u32[]{:S(2)}, u32[]{:S(2)}) collective-permute-start(f32[2,22,1,256]{3,1,2,0:T(8,128)S(1)} %copy.72), channel_id=1, source_target_pairs={{0,4},{4,8},{8,12},{1,5},{5,9},{9,13},{2,6},{6,10},{10,14},{3,7},{... | collective-permute-start | bytes 135176 | tf_op jit(solution)/shard_map/ppermute | solution.py:23
  15.2 1.6 %collective-permute-done.3 = f32[2,22,1,256]{3,1,2,0:T(8,128)S(1)} collective-permute-done((f32[2,22,1,256]{3,1,2,0:T(8,128)S(1)}, f32[2,22,1,256]{3,1,2,0:T(8,128)S(1)}, u32[]{:S(2)}, u32[]{:S(2)}) %collective-permute-start.3) | collective-permute-done | bytes 45088 | tf_op jit(solution)/shard_map/ppermute | solution.py:23
  18.1 3.8 %collective-permute-start.5 = (f32[2,22,26,1]{2,1,3,0:T(8,128)S(1)}, f32[2,22,26,1]{2,1,3,0:T(8,128)S(1)}, u32[]{:S(2)}, u32[]{:S(2)}) collective-permute-start(f32[2,22,26,1]{2,1,3,0:T(8,128)S(1)} %copy.59), channel_id=1, source_target_pairs={{0,2},{1,3},{4,6},{5,7},{8,10},{9,11},{12,14},{13,15},{16,18},{17,... | collective-permute-start | bytes 13736 | tf_op jit(solution)/shard_map/ppermute | solution.py:23
  21.9 1.3 %collective-permute-start.4 = (f32[2,22,26,1]{2,1,3,0:T(8,128)S(1)}, f32[2,22,26,1]{2,1,3,0:T(8,128)S(1)}, u32[]{:S(2)}, u32[]{:S(2)}) collective-permute-start(f32[2,22,26,1]{2,1,3,0:T(8,128)S(1)} %copy.57), channel_id=1, source_target_pairs={{2,0},{3,1},{6,4},{7,5},{10,8},{11,9},{14,12},{15,13},{18,16},{19,... | collective-permute-start | bytes 13736 | tf_op jit(solution)/shard_map/ppermute | solution.py:24
  23.2 1.9 %pad_maximum_fusion.2 = (f32[2,22,25,256]{3,2,1,0:T(8,128)}, f32[2,22,25,256]{3,2,1,0:T(8,128)}) fusion(f32[2,22,1,256]{3,2,1,0:T(1,128)S(1)} %copy.52, f32[2,1,24,256]{3,2,1,0:T(8,128)S(1)} %collective-permute-done.1, f32[2,20,24,256]{3,2,1,0:T(8,128)S(1)} %multiply_multiply_fusion.3, f32[2,1,24,256]{3,2,1,0:T(8,128)S(1)} %collective-permute-done, ...), kind=kLoop, calls=%fused_computation.10 | loop fusion | flops 1689600 | bytes 3424256 | tf_op jit(solution)/shard_map/concatenate | solution.py:25
  25.1 2.5 %collective-permute-done.4 = f32[2,22,26,1]{2,1,3,0:T(8,128)S(1)} collective-permute-done((f32[2,22,26,1]{2,1,3,0:T(8,128)S(1)}, f32[2,22,26,1]{2,1,3,0:T(8,128)S(1)}, u32[]{:S(2)}, u32[]{:S(2)}) %collective-permute-start.4) | collective-permute-done | bytes 4608 | tf_op jit(solution)/shard_map/ppermute | solution.py:24
  29.3 2.8 %pad_maximum_fusion = (f32[2,22,26,257]{3,2,1,0:T(8,128)S(1)}, f32[2,22,26,257]{3,2,1,0:T(8,128)S(1)}) fusion(f32[2,22,26,1]{3,2,1,0:T(8,128)S(1)} %copy.58, f32[2,22,1,256]{3,2,1,0:T(1,128)S(1)} %copy.52, f32[2,1,24,256]{3,2,1,0:T(8,128)S(1)} %collective-permute-done.1, f32[2,20,24,256]{3,2,1,0:T(8,128)S(1)} %multiply_multiply_fusion.3, ...), kind=kLoop, calls=%fused_computation.6 | loop fusion | flops 2940080 | bytes 3532672 | tf_op jit(solution)/shard_map/concatenate | solution.py:25
  32.2 3.1 %multiply_multiply_fusion.1 = (f32[2,20,24,256]{3,2,1,0:T(8,128)S(1)}, f32[2,20,24,256]{3,2,1,0:T(8,128)S(1)}) fusion(f32[2,24,256]{2,1,0:T(8,128)S(1)} %multiply_add_fusion.1, f32[20,24,256]{2,1,0:T(8,128)S(1)} %broadcast_multiply_fusion, f32[2,22,26,257]{3,2,1,0:T(8,128)S(1)} %get-tuple-element.26, f32[2,22,26,257]{3,2,1,0:T(8,128)S(1)} %get-tuple-element.25, ...), kind=kLoop, calls=%fused_computation.1 | loop fusion | flops 6881280 | bytes 16367616 | tf_op jit(solution)/shard_map/mul | solution.py:54
  37.3 1.3 %collective-permute-start.7 = (f32[2,1,24,256]{3,2,1,0:T(8,128)}, f32[2,1,24,256]{3,2,1,0:T(8,128)}, u32[]{:S(2)}, u32[]{:S(2)}) collective-permute-start(f32[2,1,24,256]{3,2,1,0:T(8,128)} %get-tuple-element.36), channel_id=1, source_target_pairs={{1,0},{3,2},{5,4},{7,6},{9,8},{11,10},{13,12},{15,14},{17,16},{19,... | collective-permute-start | bytes 147464 | tf_op jit(solution)/shard_map/ppermute | solution.py:24
  39.2 13.4 %all-reduce.3 = (f32[2]{0:T(128)S(1)}, f32[2]{0:T(128)}) all-reduce(f32[2]{0:T(128)S(1)} %get-tuple-element.6, f32[2]{0:T(128)S(1)} %get-tuple-element.5), channel_id=1, replica_groups=mesh['group'=2,'tile'=4,'col'=2,'layer'=2] {'tile'}, use_global_device_ids=true, to_apply=%region_1.0 | all-reduce | flops 4 | bytes 32 | tf_op jit(solution)/shard_map/psum | solution.py:83
  52.6 5.9 %all-reduce.1 = (f32[2]{0:T(128)S(1)}, f32[2]{0:T(128)S(1)}) all-reduce(f32[2]{0:T(128)S(1)} %get-tuple-element.13, f32[2]{0:T(128)} %get-tuple-element.14), channel_id=1, replica_groups=mesh['group'=2,'tile'=4,'col'=2,'layer'=2] {'col','layer'}, use_global_device_ids=true, to_apply=%region_2.0 | all-reduce | flops 4 | bytes 32 | tf_op jit(solution)/shard_map/psum | solution.py:82
  59.3 1.3 %collective-permute-start.8 = (f32[2,22,1,256]{3,1,2,0:T(8,128)S(1)}, f32[2,22,1,256]{3,1,2,0:T(8,128)S(1)}, u32[]{:S(2)}, u32[]{:S(2)}) collective-permute-start(f32[2,22,1,256]{3,1,2,0:T(8,128)S(1)} %copy.73), channel_id=1, source_target_pairs={{4,0},{8,4},{12,8},{5,1},{9,5},{13,9},{6,2},{10,6},{14,10},{7,3},{... | collective-permute-start | bytes 135176 | tf_op jit(solution)/shard_map/ppermute | solution.py:24
  60.6 4.5 %collective-permute-start.9 = (f32[2,22,1,256]{3,1,2,0:T(8,128)S(1)}, f32[2,22,1,256]{3,1,2,0:T(8,128)S(1)}, u32[]{:S(2)}, u32[]{:S(2)}) collective-permute-start(f32[2,22,1,256]{3,1,2,0:T(8,128)S(1)} %copy.74), channel_id=1, source_target_pairs={{0,4},{4,8},{8,12},{1,5},{5,9},{9,13},{2,6},{6,10},{10,14},{3,7},{... | collective-permute-start | bytes 135176 | tf_op jit(solution)/shard_map/ppermute | solution.py:23
  68.0 1.3 %fusion.23 = (f32[2,22,26,1]{3,2,1,0:T(8,128)}, f32[2,22,26,1]{3,2,1,0:T(8,128)}) fusion(f32[2,22,26,256]{3,2,1,0:T(8,128)S(1)} %pad_maximum_fusion.5), kind=kLoop, calls=%fused_computation.76 | loop fusion | bytes 18304 | tf_op jit(solution)/shard_map/slice | solution.py:22
  69.4 2.1 %copy.67 = f32[2,22,26,1]{2,1,3,0:T(8,128)} copy(f32[2,22,26,1]{3,2,1,0:T(8,128)} %get-tuple-element.19) | data formatting | bytes 9152 | tf_op jit(solution)/shard_map/slice | solution.py:22
  71.5 2.1 %copy.69 = f32[2,22,26,1]{2,1,3,0:T(8,128)} copy(f32[2,22,26,1]{3,2,1,0:T(8,128)} %get-tuple-element.20) | data formatting | bytes 9152 | tf_op jit(solution)/shard_map/slice | solution.py:21
  73.6 3.7 %collective-permute-start.11 = (f32[2,22,26,1]{2,1,3,0:T(8,128)}, f32[2,22,26,1]{2,1,3,0:T(8,128)}, u32[]{:S(2)}, u32[]{:S(2)}) collective-permute-start(f32[2,22,26,1]{2,1,3,0:T(8,128)} %copy.69), channel_id=1, source_target_pairs={{0,2},{1,3},{4,6},{5,7},{8,10},{9,11},{12,14},{13,15},{16,18},{17,... | collective-permute-start | bytes 13736 | tf_op jit(solution)/shard_map/ppermute | solution.py:23
  77.3 1.3 %collective-permute-start.10 = (f32[2,22,26,1]{2,1,3,0:T(8,128)}, f32[2,22,26,1]{2,1,3,0:T(8,128)}, u32[]{:S(2)}, u32[]{:S(2)}) collective-permute-start(f32[2,22,26,1]{2,1,3,0:T(8,128)} %copy.67), channel_id=1, source_target_pairs={{2,0},{3,1},{6,4},{7,5},{10,8},{11,9},{14,12},{15,13},{18,16},{19,... | collective-permute-start | bytes 13736 | tf_op jit(solution)/shard_map/ppermute | solution.py:24
  78.6 2.8 %pad_maximum_fusion.4 = (f32[2,22,25,256]{3,2,1,0:T(8,128)}, f32[2,22,25,256]{3,2,1,0:T(8,128)}) fusion(f32[2,22,1,256]{3,2,1,0:T(1,128)} %copy-done.8, f32[2,1,24,256]{3,2,1,0:T(8,128)} %collective-permute-done.7, f32[2,20,24,256]{3,2,1,0:T(8,128)S(1)} %get-tuple-element.17, f32[2,1,24,256]{3,2,1,0:T(8,128)S(1)} %collective-permute-done.6, ...), kind=kLoop, calls=%fused_computation.13 | loop fusion | flops 1689600 | bytes 3424256 | tf_op jit(solution)/shard_map/concatenate | solution.py:25
  81.4 1.9 %collective-permute-done.10 = f32[2,22,26,1]{2,1,3,0:T(8,128)} collective-permute-done((f32[2,22,26,1]{2,1,3,0:T(8,128)}, f32[2,22,26,1]{2,1,3,0:T(8,128)}, u32[]{:S(2)}, u32[]{:S(2)}) %collective-permute-start.10) | collective-permute-done | bytes 4608 | tf_op jit(solution)/shard_map/ppermute | solution.py:24
  83.3 2.0 %copy.68 = f32[2,22,26,1]{3,2,1,0:T(8,128)} copy(f32[2,22,26,1]{2,1,3,0:T(8,128)} %collective-permute-done.10) | data formatting | bytes 9152 | tf_op jit(solution)/shard_map/ppermute | solution.py:24
  85.3 2.0 %copy.70 = f32[2,22,26,1]{3,2,1,0:T(8,128)} copy(f32[2,22,26,1]{2,1,3,0:T(8,128)} %collective-permute-done.11) | data formatting | bytes 9152 | tf_op jit(solution)/shard_map/ppermute | solution.py:23
  87.3 3.1 %pad_maximum_fusion.1 = (f32[2,22,26,257]{3,2,1,0:T(8,128)S(1)}, f32[2,22,26,257]{3,2,1,0:T(8,128)S(1)}) fusion(f32[2,22,26,1]{3,2,1,0:T(8,128)} %copy.68, f32[2,22,1,256]{3,2,1,0:T(1,128)} %copy-done.8, f32[2,1,24,256]{3,2,1,0:T(8,128)} %collective-permute-done.7, f32[2,20,24,256]{3,2,1,0:T(8,128)S(1)} %get-tuple-element.17, ...), kind=kLoop, calls=%fused_computation.8 | loop fusion | flops 2940080 | bytes 3532672 | tf_op jit(solution)/shard_map/concatenate | solution.py:25
  90.4 3.5 %fusion.11 = f32[2]{0:T(128)S(1)} fusion(f32[2,20,24,256]{3,2,1,0:T(8,128)S(1)} %copy-done.2, f32[2,22,26,257]{3,2,1,0:T(8,128)S(1)} %get-tuple-element.24, f32[2,22,26,257]{3,2,1,0:T(8,128)S(1)} %get-tuple-element.23, f32[2,22,25,256]{3,2,1,0:T(8,128)S(1)} %copy-done.6, f32[2,22,25,256]{3,2,1,0:T(8,128)S(1)} %copy-done.5, ...), kind=kLoop, calls=%fused_computation.27 | loop fusion | flops 8110078 | bytes 15384592 | tf_op jit(solution)/shard_map/reduce_sum | solution.py:86
  93.9 10.7 %all-reduce.2 = (f32[2]{0:T(128)S(1)}, f32[2]{0:T(128)S(1)}) all-reduce(f32[2]{0:T(128)S(1)} %multiply_reduce_fusion, f32[2]{0:T(128)S(1)} %fusion.11), channel_id=1, replica_groups=mesh['group'=2,'tile'=4,'col'=2,'layer'=2] {'tile'}, use_global_device_ids=true, to_apply=%region_7.0 | all-reduce | flops 4 | bytes 32 | tf_op jit(solution)/shard_map/psum | solution.py:83
  104.5 5.6 %all-reduce = (f32[2]{0:T(128)S(1)}, f32[2]{0:T(128)S(1)}) all-reduce(f32[2]{0:T(128)S(1)} %get-tuple-element.11, f32[2]{0:T(128)S(1)} %get-tuple-element.12), channel_id=1, replica_groups=mesh['group'=2,'tile'=4,'col'=2,'layer'=2] {'col','layer'}, use_global_device_ids=true, to_apply=%region_8.0 | all-reduce | flops 4 | bytes 32 | tf_op jit(solution)/shard_map/psum | solution.py:82
  110.9 1.4 %multiply_add_fusion = f32[2,20,24,256]{3,2,1,0:T(8,128)} fusion(f32[2]{0:T(128)S(1)} %get-tuple-element.16, f32[2]{0:T(128)S(1)} %get-tuple-element.15, f32[2]{0:T(128)S(1)} %div.19, f32[2,20,24,256]{3,2,1,0:T(8,128)S(1)} %copy-done.2, f32[2,24,256]{2,1,0:T(8,128)S(1)} %multiply_add_fusion.1, f32[20,24,256]{2,1,0:T(8,128)S(1)} %broadcast_multiply_fusion, ...), kind=kLoop, calls=%fused_computation.62 | loop fusion | flops 3440640 | bytes 3489816 | tf_op jit(solution)/shard_map/add | solution.py:99
  (56 shorter events, 11.8 us)
Async XLA Ops:
  3.1 3.7 %collective-permute-start = (f32[2,1,24,256]{3,2,1,0:T(8,128)S(1)}, f32[2,1,24,256]{3,2,1,0:T(8,128)S(1)}, u32[]{:S(2)}, u32[]{:S(2)}) collective-permute-start(f32[2,1,24,256]{3,2,1,0:T(8,128)S(1)} %get-tuple-element.37), channel_id=1, source_target_pairs={{0,1},{2,3},{4,5},{6,7},{8,9},{10,11},{12,13},{14,15},{16,17},{18,... | collective-permute-start | bytes 147464 | tf_op jit(solution)/shard_map/ppermute | solution.py:23
  5.5 3.1 %collective-permute-start.1 = (f32[2,1,24,256]{3,2,1,0:T(8,128)S(1)}, f32[2,1,24,256]{3,2,1,0:T(8,128)S(1)}, u32[]{:S(2)}, u32[]{:S(2)}) collective-permute-start(f32[2,1,24,256]{3,2,1,0:T(8,128)S(1)} %get-tuple-element.38), channel_id=1, source_target_pairs={{1,0},{3,2},{5,4},{7,6},{9,8},{11,10},{13,12},{15,14},{17,16},{19,... | collective-permute-start | bytes 147464 | tf_op jit(solution)/shard_map/ppermute | solution.py:24
  8.7 20.6 %copy-start.7 = (f32[2,1,24,256]{3,2,1,0:T(8,128)}, f32[2,1,24,256]{3,2,1,0:T(8,128)S(1)}, u32[]{:S(2)}) copy-start(f32[2,1,24,256]{3,2,1,0:T(8,128)S(1)} %collective-permute-done.1) | copy-start | bytes 147460
  8.8 6.4 %collective-permute-start.2 = (f32[2,22,1,256]{3,1,2,0:T(8,128)S(1)}, f32[2,22,1,256]{3,1,2,0:T(8,128)S(1)}, u32[]{:S(2)}, u32[]{:S(2)}) collective-permute-start(f32[2,22,1,256]{3,1,2,0:T(8,128)S(1)} %copy.71), channel_id=1, source_target_pairs={{4,0},{8,4},{12,8},{5,1},{9,5},{13,9},{6,2},{10,6},{14,10},{7,3},{... | collective-permute-start | bytes 135176 | tf_op jit(solution)/shard_map/ppermute | solution.py:24
  10.1 6.7 %collective-permute-start.3 = (f32[2,22,1,256]{3,1,2,0:T(8,128)S(1)}, f32[2,22,1,256]{3,1,2,0:T(8,128)S(1)}, u32[]{:S(2)}, u32[]{:S(2)}) collective-permute-start(f32[2,22,1,256]{3,1,2,0:T(8,128)S(1)} %copy.72), channel_id=1, source_target_pairs={{0,4},{4,8},{8,12},{1,5},{5,9},{9,13},{2,6},{6,10},{10,14},{3,7},{... | collective-permute-start | bytes 135176 | tf_op jit(solution)/shard_map/ppermute | solution.py:23
  18.1 10.0 %collective-permute-start.5 = (f32[2,22,26,1]{2,1,3,0:T(8,128)S(1)}, f32[2,22,26,1]{2,1,3,0:T(8,128)S(1)}, u32[]{:S(2)}, u32[]{:S(2)}) collective-permute-start(f32[2,22,26,1]{2,1,3,0:T(8,128)S(1)} %copy.59), channel_id=1, source_target_pairs={{0,2},{1,3},{4,6},{5,7},{8,10},{9,11},{12,14},{13,15},{16,18},{17,... | collective-permute-start | bytes 13736 | tf_op jit(solution)/shard_map/ppermute | solution.py:23
  21.9 5.7 %collective-permute-start.4 = (f32[2,22,26,1]{2,1,3,0:T(8,128)S(1)}, f32[2,22,26,1]{2,1,3,0:T(8,128)S(1)}, u32[]{:S(2)}, u32[]{:S(2)}) collective-permute-start(f32[2,22,26,1]{2,1,3,0:T(8,128)S(1)} %copy.57), channel_id=1, source_target_pairs={{2,0},{3,1},{6,4},{7,5},{10,8},{11,9},{14,12},{15,13},{18,16},{19,... | collective-permute-start | bytes 13736 | tf_op jit(solution)/shard_map/ppermute | solution.py:24
  29.3 2.8 %copy-start = (f32[2,20,24,256]{3,2,1,0:T(8,128)S(1)}, f32[2,20,24,256]{3,2,1,0:T(8,128)}, u32[]{:S(2)}) copy-start(f32[2,20,24,256]{3,2,1,0:T(8,128)} %param.4) | copy-start | bytes 2949124
  29.3 2.9 %copy-start.3 = (f32[2,22,25,256]{3,2,1,0:T(8,128)S(1)}, f32[2,22,25,256]{3,2,1,0:T(8,128)}, u32[]{:S(2)}) copy-start(f32[2,22,25,256]{3,2,1,0:T(8,128)} %get-tuple-element.31) | copy-start | bytes 3379204
  29.3 2.9 %copy-start.4 = (f32[2,22,25,256]{3,2,1,0:T(8,128)S(1)}, f32[2,22,25,256]{3,2,1,0:T(8,128)}, u32[]{:S(2)}) copy-start(f32[2,22,25,256]{3,2,1,0:T(8,128)} %get-tuple-element.32) | copy-start | bytes 3379204
  35.3 3.3 %copy-start.1 = (f32[2,20,24,256]{3,2,1,0:T(8,128)}, f32[2,20,24,256]{3,2,1,0:T(8,128)S(1)}, u32[]{:S(2)}) copy-start(f32[2,20,24,256]{3,2,1,0:T(8,128)S(1)} %get-tuple-element.18) | copy-start | bytes 2949124
  36.0 22.5 %collective-permute-start.6 = (f32[2,1,24,256]{3,2,1,0:T(8,128)}, f32[2,1,24,256]{3,2,1,0:T(8,128)S(1)}, u32[]{:S(2)}, u32[]{:S(2)}) collective-permute-start(f32[2,1,24,256]{3,2,1,0:T(8,128)} %get-tuple-element.35), channel_id=1, source_target_pairs={{0,1},{2,3},{4,5},{6,7},{8,9},{10,11},{12,13},{14,15},{16,17},{18,... | collective-permute-start | bytes 147464 | tf_op jit(solution)/shard_map/ppermute | solution.py:23
  37.3 21.2 %collective-permute-start.7 = (f32[2,1,24,256]{3,2,1,0:T(8,128)}, f32[2,1,24,256]{3,2,1,0:T(8,128)}, u32[]{:S(2)}, u32[]{:S(2)}) collective-permute-start(f32[2,1,24,256]{3,2,1,0:T(8,128)} %get-tuple-element.36), channel_id=1, source_target_pairs={{1,0},{3,2},{5,4},{7,6},{9,8},{11,10},{13,12},{15,14},{17,16},{19,... | collective-permute-start | bytes 147464 | tf_op jit(solution)/shard_map/ppermute | solution.py:24
  39.2 25.9 %copy-start.2 = (f32[2,20,24,256]{3,2,1,0:T(8,128)S(1)}, f32[2,20,24,256]{3,2,1,0:T(8,128)}, u32[]{:S(2)}) copy-start(f32[2,20,24,256]{3,2,1,0:T(8,128)} %copy-done.1) | copy-start | bytes 2949124
  58.5 7.3 %copy-start.10 = (f32[2]{0:T(128)}, f32[2]{0:T(128)S(1)}, u32[]{:S(2)}) copy-start(f32[2]{0:T(128)S(1)} %get-tuple-element.10) | copy-start | bytes 28
  59.3 6.4 %collective-permute-start.8 = (f32[2,22,1,256]{3,1,2,0:T(8,128)S(1)}, f32[2,22,1,256]{3,1,2,0:T(8,128)S(1)}, u32[]{:S(2)}, u32[]{:S(2)}) collective-permute-start(f32[2,22,1,256]{3,1,2,0:T(8,128)S(1)} %copy.73), channel_id=1, source_target_pairs={{4,0},{8,4},{12,8},{5,1},{9,5},{13,9},{6,2},{10,6},{14,10},{7,3},{... | collective-permute-start | bytes 135176 | tf_op jit(solution)/shard_map/ppermute | solution.py:24
  60.6 6.3 %collective-permute-start.9 = (f32[2,22,1,256]{3,1,2,0:T(8,128)S(1)}, f32[2,22,1,256]{3,1,2,0:T(8,128)S(1)}, u32[]{:S(2)}, u32[]{:S(2)}) collective-permute-start(f32[2,22,1,256]{3,1,2,0:T(8,128)S(1)} %copy.74), channel_id=1, source_target_pairs={{0,4},{4,8},{8,12},{1,5},{5,9},{9,13},{2,6},{6,10},{10,14},{3,7},{... | collective-permute-start | bytes 135176 | tf_op jit(solution)/shard_map/ppermute | solution.py:23
  65.8 3.6 %copy-start.8 = (f32[2,22,1,256]{3,2,1,0:T(1,128)}, f32[2,22,1,256]{3,2,1,0:T(1,128)S(1)}, u32[]{:S(2)}) copy-start(f32[2,22,1,256]{3,2,1,0:T(1,128)S(1)} %copy.62) | copy-start | bytes 135172
  67.0 2.4 %copy-start.9 = (f32[2,22,1,256]{3,2,1,0:T(1,128)}, f32[2,22,1,256]{3,2,1,0:T(1,128)S(1)}, u32[]{:S(2)}) copy-start(f32[2,22,1,256]{3,2,1,0:T(1,128)S(1)} %copy.64) | copy-start | bytes 135172
  73.6 11.7 %collective-permute-start.11 = (f32[2,22,26,1]{2,1,3,0:T(8,128)}, f32[2,22,26,1]{2,1,3,0:T(8,128)}, u32[]{:S(2)}, u32[]{:S(2)}) collective-permute-start(f32[2,22,26,1]{2,1,3,0:T(8,128)} %copy.69), channel_id=1, source_target_pairs={{0,2},{1,3},{4,6},{5,7},{8,10},{9,11},{12,14},{13,15},{16,18},{17,... | collective-permute-start | bytes 13736 | tf_op jit(solution)/shard_map/ppermute | solution.py:23
  77.3 6.0 %collective-permute-start.10 = (f32[2,22,26,1]{2,1,3,0:T(8,128)}, f32[2,22,26,1]{2,1,3,0:T(8,128)}, u32[]{:S(2)}, u32[]{:S(2)}) collective-permute-start(f32[2,22,26,1]{2,1,3,0:T(8,128)} %copy.67), channel_id=1, source_target_pairs={{2,0},{3,1},{6,4},{7,5},{10,8},{11,9},{14,12},{15,13},{18,16},{19,... | collective-permute-start | bytes 13736 | tf_op jit(solution)/shard_map/ppermute | solution.py:24
  87.3 3.1 %copy-start.5 = (f32[2,22,25,256]{3,2,1,0:T(8,128)S(1)}, f32[2,22,25,256]{3,2,1,0:T(8,128)}, u32[]{:S(2)}) copy-start(f32[2,22,25,256]{3,2,1,0:T(8,128)} %get-tuple-element.27) | copy-start | bytes 3379204
  87.3 3.1 %copy-start.6 = (f32[2,22,25,256]{3,2,1,0:T(8,128)S(1)}, f32[2,22,25,256]{3,2,1,0:T(8,128)}, u32[]{:S(2)}) copy-start(f32[2,22,25,256]{3,2,1,0:T(8,128)} %get-tuple-element.28) | copy-start | bytes 3379204
